TPU v7x, 256 devices: a whole 4x4x8 slice. The times are simulated.
256 devices in a mesh: fx: 32 (over z, x), fy: 8 (over y, core).
Axes of the slice: x: 4, y: 4, z: 8, core: 2. Of those that a mesh axis runs over, the one named last changes fastest.
Arguments:
- right_side: float32 [4096, 2048], P(('fx', 'fy'))
- coupling: float32 [4096, 11, 4096], P(('fx', 'fy')), may hold values from -0.109375 to 0.109375
- face_columns: int32 [4096, 11], P(('fx', 'fy')), may hold values from 0 to 31, as said below
- ghost_lists: int32 [1024, 4], P(('fx', 'fy')), may hold values from 0 to 15, as said below
Outputs:
- solution: float32 [4096, 2048], P(('fx', 'fy'))
- residual: float32 [4096, 2048], P(('fx', 'fy'))
Inputs may be any that keep to these rules, and one draw needn't show every extreme that they name: face_columns[f, 0] is f's own index within its block; entries 1 to 6 name other faces of the same block, all distinct and below 16; entries 7 to 10 are distinct and name received faces, 16 + d * 4 + g for the g-th face of group d of the extended list; every received slot of every block is named by some row of that block. `ghost_lists`: each row names 4 distinct faces of its block by local index.
All inputs are finite; a program needn't handle non-finite values.
Results may differ from a plain program's by a relative error of at most 0.0003.
Values sent between devices are 32-bit elements; how exact they have to be, the bound alone decides.
No kernel may reach another device: no remote copies, remote signals or barrier semaphores. Data moves between devices by JAX's collectives and lax.ppermute only.
A program may use at most 64 MiB of HBM per device.

v0:
```python
import jax
import jax.numpy as jnp
from jax import lax
from jax.sharding import PartitionSpec as P

DOF = 64
NRHS = 32
BLOCKS = 11
POWERS = 3


def from_behind(block, axis, distance):
    devices = range(lax.axis_size(axis))
    route = [(i - distance, i) for i in devices if i - distance in devices]
    return lax.ppermute(block, axis, route)


def receive_rows(field, ghost_lists):
    from_lower_x = from_behind(jnp.take(field, ghost_lists[1], axis=0), "fx", 1)
    from_upper_x = from_behind(jnp.take(field, ghost_lists[0], axis=0), "fx", -1)
    from_lower_y = from_behind(jnp.take(field, ghost_lists[3], axis=0), "fy", 1)
    from_upper_y = from_behind(jnp.take(field, ghost_lists[2], axis=0), "fy", -1)
    return jnp.concatenate([from_lower_x, from_upper_x, from_lower_y, from_upper_y], axis=0)


def contract(block_mats, picked):
    face_count = picked.shape[0]
    shaped = picked.reshape(face_count, picked.shape[1], DOF, NRHS)
    result = jnp.einsum("fkab,fkbr->far", block_mats, shaped, precision=lax.Precision.HIGHEST)
    return result.reshape(face_count, DOF * NRHS)


def solve_small(gram_total):
    count = NRHS
    row_ids = jnp.arange((POWERS + 1) * count)[:, None]
    col_ids = jnp.arange(POWERS * count)[None, :]
    shift_map = ((row_ids == col_ids) | (row_ids == col_ids + count)).astype(jnp.float32)
    first = (row_ids == jnp.arange(count)[None, :]).astype(jnp.float32)
    high = lax.Precision.HIGHEST
    normal_matrix = jnp.dot(
        shift_map.T, jnp.dot(gram_total, shift_map, precision=high), precision=high
    )
    right_terms = jnp.dot(shift_map.T, gram_total[:, :count], precision=high)
    factor = jnp.linalg.cholesky(normal_matrix)
    coeffs = jax.scipy.linalg.cho_solve((factor, True), right_terms)
    combo = first - jnp.dot(shift_map, coeffs, precision=high)
    return (coeffs, combo)


def on_device(right_side, coupling, face_columns, ghost_lists):
    face_count = right_side.shape[0]
    block_mats = coupling.reshape(face_count, BLOCKS, DOF, DOF)
    high = lax.Precision.HIGHEST

    def as_rows(field):
        return field.reshape(face_count * DOF, NRHS)

    fields = [right_side]
    for power_index in range(POWERS):
        power_field = fields[-1]
        received = receive_rows(power_field, ghost_lists)
        extended = jnp.concatenate([power_field, received], axis=0)
        fields.append(contract(block_mats, jnp.take(extended, face_columns, axis=0)))
    stacked = jnp.concatenate([as_rows(item) for item in fields], axis=1)
    local_gram = jnp.dot(stacked.T, stacked, precision=high, preferred_element_type=jnp.float32)
    gram_total = lax.psum(local_gram, ("fx", "fy"))
    coeffs, combo = solve_small(gram_total)
    solution = jnp.dot(stacked[:, : POWERS * NRHS], coeffs, precision=high)
    residual = jnp.dot(stacked, combo, precision=high)
    return (solution.reshape(face_count, DOF * NRHS), residual.reshape(face_count, DOF * NRHS))


def solution(mesh):
    placed = (
        P(("fx", "fy"), None),
        P(("fx", "fy"), None, None),
        P(("fx", "fy"), None),
        P(("fx", "fy"), None),
    )
    return jax.shard_map(
        on_device,
        mesh=mesh,
        in_specs=placed,
        out_specs=(P(("fx", "fy"), None), P(("fx", "fy"), None)),
        check_vma=False,
    )
```

profile of v0, /device:TPU:1, one launch (start us, length us, event | category | flops | bytes accessed | tf_op | source)
XLA Modules:
  0.0 415.1 jit_solution(4617153673329050650)
XLA Ops:
  7.2 0.8 compare_and_fusion.1
  8.1 1.5 gather_fusion
  9.6 3.9 collective-permute-start
  13.6 1.5 gather_fusion.1
  15.2 1.3 collective-permute-start.1
  16.5 1.5 gather_fusion.2
  18.0 4.0 collective-permute-start.2
  22.1 1.5 gather_fusion.3
  23.7 1.9 collective-permute-start.3
  25.6 0.7 compare_select_fusion
  26.3 0.7 compare_and_fusion
  27.1 5.7 %reshape.61 = f32[16,11,64,64]{3,2,0,1:T(8,128)} reshape(f32[16,11,4096]{2,0,1:T(8,128)} %param.9) | data formatting | bytes 5767168 | tf_op jit(solution)/shard_map/reshape | solution.py:52
  32.9 1.2 gather_fusion.4
  34.1 1.5 reshape.217
  35.6 1.8 broadcast_select_fusion.2
  37.4 3.6 reshape.245
  41.0 12.0 %fusion.6 = f32[16,64,32]{1,2,0:T(8,128)S(1)} fusion(f32[16,11,64,64]{3,2,0,1:T(8,128)} %reshape.61, f32[16,11,64,32]{3,2,1,0:T(8,128)} %reshape.245), kind=kOutput, calls=%fused_computation.21 | convolution fusion | flops 276824064 | bytes 4456448 | tf_op jit(solution)/shard_map/fkab,fkbr->far/dot_general | solution.py:29
  53.0 0.2 copy.50
  53.2 0.2 reshape.62
  53.4 0.6 gather_fusion.6
  54.0 0.6 gather_fusion.7
  54.6 0.6 gather_fusion.8
  55.2 0.6 gather_fusion.5
  55.8 1.3 collective-permute-start.5
  57.2 3.6 collective-permute-start.6
  60.9 1.9 collective-permute-start.7
  62.9 5.1 %collective-permute-start.4 = (f32[4,2048]{1,0:T(4,128)S(1)}, f32[4,2048]{1,0:T(4,128)S(1)}, u32[]{:S(2)}, u32[]{:S(2)}) collective-permute-start(f32[4,2048]{1,0:T(4,128)S(1)} %broadcast_select_fusion.10), channel_id=1, source_target_pairs={{0,8},{8,16},{16,24},{24,32},{32,40},{40,48},{48,56},{56,64},{64,7... | collective-permute-start | bytes 98312 | tf_op jit(solution)/shard_map/ppermute | solution.py:15
  68.0 0.8 collective-permute-done.4
  68.9 1.2 gather_fusion.9
  70.0 1.6 reshape.229
  71.7 3.2 broadcast_select_fusion.1
  74.9 5.2 %reshape.246 = f32[16,11,64,32]{3,2,1,0:T(8,128)} reshape(f32[16,11,2048]{2,1,0:T(8,128)} %broadcast_select_fusion.1) | data formatting | bytes 2883584 | tf_op jit(solution)/shard_map/reshape | solution.py:28
  80.1 12.0 %fusion.9 = f32[16,64,32]{1,2,0:T(8,128)S(1)} fusion(f32[16,11,64,64]{3,2,0,1:T(8,128)} %reshape.61, f32[16,11,64,32]{3,2,1,0:T(8,128)} %reshape.246), kind=kOutput, calls=%fused_computation.22 | convolution fusion | flops 276824064 | bytes 4456448 | tf_op jit(solution)/shard_map/fkab,fkbr->far/dot_general | solution.py:29
  92.3 0.2 reshape.64
  92.6 0.6 gather_fusion.12
  93.1 0.6 gather_fusion.13
  93.7 0.6 gather_fusion.11
  94.3 0.6 gather_fusion.10
  94.9 4.5 %collective-permute-start.10 = (f32[4,2048]{1,0:T(4,128)S(1)}, f32[4,2048]{1,0:T(4,128)S(1)}, u32[]{:S(2)}, u32[]{:S(2)}) collective-permute-start(f32[4,2048]{1,0:T(4,128)S(1)} %broadcast_select_fusion.4), channel_id=1, source_target_pairs={{0,1},{1,2},{2,3},{3,4},{4,5},{5,6},{6,7},{8,9},{9,10},{10,11},{11... | collective-permute-start | bytes 98312 | tf_op jit(solution)/shard_map/ppermute | solution.py:15
  99.5 1.9 collective-permute-start.11
  101.5 1.3 collective-permute-start.9
  102.9 4.8 %collective-permute-start.8 = (f32[4,2048]{1,0:T(4,128)S(1)}, f32[4,2048]{1,0:T(4,128)S(1)}, u32[]{:S(2)}, u32[]{:S(2)}) collective-permute-start(f32[4,2048]{1,0:T(4,128)S(1)} %broadcast_select_fusion.6), channel_id=1, source_target_pairs={{0,8},{8,16},{16,24},{24,32},{32,40},{40,48},{48,56},{56,64},{64,7... | collective-permute-start | bytes 98312 | tf_op jit(solution)/shard_map/ppermute | solution.py:15
  107.9 0.6 collective-permute-done.8
  108.5 1.2 gather_fusion.14
  109.7 1.6 reshape.241
  111.3 3.2 broadcast_select_fusion
  114.6 5.2 %reshape.247 = f32[16,11,64,32]{3,2,1,0:T(8,128)} reshape(f32[16,11,2048]{2,1,0:T(8,128)} %broadcast_select_fusion) | data formatting | bytes 2883584 | tf_op jit(solution)/shard_map/reshape | solution.py:28
  119.7 12.3 %fusion.12 = f32[16,64,32]{1,2,0:T(8,128)S(1)} fusion(f32[16,11,64,64]{3,2,0,1:T(8,128)} %reshape.61, f32[16,11,64,32]{3,2,1,0:T(8,128)} %reshape.247), kind=kOutput, calls=%fused_computation.23 | convolution fusion | flops 276824064 | bytes 4456448 | tf_op jit(solution)/shard_map/fkab,fkbr->far/dot_general | solution.py:29
  132.2 0.5 pad_maximum_fusion
  132.7 1.6 fusion.37
  134.4 250.2 %all-reduce.2.cloned.1.call-done = f32[128,128]{1,0:T(8,128)} async-done(((f32[128,128]{1,0:T(8,128)}), f32[128,128]{1,0:T(8,128)}) %all-reduce.2.cloned.1.call-update) | async-done | bytes 65552 | tf_op jit(solution)/shard_map/psum | solution.py:66
  384.6 1.0 fusion.34
  385.6 0.2 fusion.32
  385.9 8.8 %cholesky.16 = f32[96,96]{1,0:T(8,128)S(1)} custom-call(f32[96,96]{1,0:T(8,128)S(1)} %fusion.29), custom_call_target="Cholesky" | custom-call | tf_op jit(solution)/shard_map/jit(cholesky)/cholesky | solution.py:44
  394.8 0.6 compare_reduce_fusion
  395.4 0.7 fusion.24
  396.1 7.4 %custom-call.10 = f32[1,96,96]{1,2,0:T(8,128)S(1)} custom-call(f32[1,96,96]{2,1,0:T(8,128)S(1)} %fusion.24), custom_call_target="InvertDiagBlocksLowerTriangular" | custom-call | tf_op jit(solution)/shard_map/jit(_cho_solve)/triangular_solve | solution.py:45
  403.4 1.1 fusion.21
  404.5 0.3 fusion.27
  404.8 0.2 fusion.25
  405.2 0.7 fusion.15
  405.9 0.6 fusion.38
  406.5 0.9 reshape.67
  407.4 0.9 reshape.66
  (43 shorter events, 2.3 us)
Async XLA Ops:
  7.2 377.4 %all-reduce.2.cloned.1.call-start = ((), (), s32[]{:S(2)}) async-start(), calls=%async_computation | async-start | bytes 131072 | tf_op jit(solution)/shard_map/psum | solution.py:66
  9.6 23.2 %collective-permute-start = (f32[4,2048]{1,0:T(4,128)S(1)}, f32[4,2048]{1,0:T(4,128)S(1)}, u32[]{:S(2)}, u32[]{:S(2)}) collective-permute-start(f32[4,2048]{1,0:T(4,128)S(1)} %broadcast_select_fusion.14), channel_id=1, source_target_pairs={{0,8},{8,16},{16,24},{24,32},{32,40},{40,48},{48,56},{56,64},{64,7... | collective-permute-start | bytes 98312 | tf_op jit(solution)/shard_map/ppermute | solution.py:15
  15.2 17.6 %collective-permute-start.1 = (f32[4,2048]{1,0:T(4,128)S(1)}, f32[4,2048]{1,0:T(4,128)S(1)}, u32[]{:S(2)}, u32[]{:S(2)}) collective-permute-start(f32[4,2048]{1,0:T(4,128)S(1)} %broadcast_select_fusion.13), channel_id=1, source_target_pairs={{8,0},{16,8},{24,16},{32,24},{40,32},{48,40},{56,48},{64,56},{72,6... | collective-permute-start | bytes 98312 | tf_op jit(solution)/shard_map/ppermute | solution.py:15
  18.0 14.8 %collective-permute-start.2 = (f32[4,2048]{1,0:T(4,128)S(1)}, f32[4,2048]{1,0:T(4,128)S(1)}, u32[]{:S(2)}, u32[]{:S(2)}) collective-permute-start(f32[4,2048]{1,0:T(4,128)S(1)} %broadcast_select_fusion.12), channel_id=1, source_target_pairs={{0,1},{1,2},{2,3},{3,4},{4,5},{5,6},{6,7},{8,9},{9,10},{10,11},{11... | collective-permute-start | bytes 98312 | tf_op jit(solution)/shard_map/ppermute | solution.py:15
  23.7 9.2 %collective-permute-start.3 = (f32[4,2048]{1,0:T(4,128)S(1)}, f32[4,2048]{1,0:T(4,128)S(1)}, u32[]{:S(2)}, u32[]{:S(2)}) collective-permute-start(f32[4,2048]{1,0:T(4,128)S(1)} %broadcast_select_fusion.11), channel_id=1, source_target_pairs={{1,0},{2,1},{3,2},{4,3},{5,4},{6,5},{7,6},{9,8},{10,9},{11,10},{12... | collective-permute-start | bytes 98312 | tf_op jit(solution)/shard_map/ppermute | solution.py:15
  27.1 5.7 %copy-start = (f32[16,2048]{1,0:T(8,128)S(1)}, f32[16,2048]{1,0:T(8,128)}, u32[]{:S(2)}) copy-start(f32[16,2048]{1,0:T(8,128)} %param.8) | copy-start | bytes 393220
  55.8 12.2 %collective-permute-start.5 = (f32[4,2048]{1,0:T(4,128)S(1)}, f32[4,2048]{1,0:T(4,128)S(1)}, u32[]{:S(2)}, u32[]{:S(2)}) collective-permute-start(f32[4,2048]{1,0:T(4,128)S(1)} %broadcast_select_fusion.9), channel_id=1, source_target_pairs={{8,0},{16,8},{24,16},{32,24},{40,32},{48,40},{56,48},{64,56},{72,6... | collective-permute-start | bytes 98312 | tf_op jit(solution)/shard_map/ppermute | solution.py:15
  57.2 10.8 %collective-permute-start.6 = (f32[4,2048]{1,0:T(4,128)S(1)}, f32[4,2048]{1,0:T(4,128)S(1)}, u32[]{:S(2)}, u32[]{:S(2)}) collective-permute-start(f32[4,2048]{1,0:T(4,128)S(1)} %broadcast_select_fusion.8), channel_id=1, source_target_pairs={{0,1},{1,2},{2,3},{3,4},{4,5},{5,6},{6,7},{8,9},{9,10},{10,11},{11... | collective-permute-start | bytes 98312 | tf_op jit(solution)/shard_map/ppermute | solution.py:15
  60.9 7.1 %collective-permute-start.7 = (f32[4,2048]{1,0:T(4,128)S(1)}, f32[4,2048]{1,0:T(4,128)S(1)}, u32[]{:S(2)}, u32[]{:S(2)}) collective-permute-start(f32[4,2048]{1,0:T(4,128)S(1)} %broadcast_select_fusion.7), channel_id=1, source_target_pairs={{1,0},{2,1},{3,2},{4,3},{5,4},{6,5},{7,6},{9,8},{10,9},{11,10},{12... | collective-permute-start | bytes 98312 | tf_op jit(solution)/shard_map/ppermute | solution.py:15
  62.9 5.9 %collective-permute-start.4 = (f32[4,2048]{1,0:T(4,128)S(1)}, f32[4,2048]{1,0:T(4,128)S(1)}, u32[]{:S(2)}, u32[]{:S(2)}) collective-permute-start(f32[4,2048]{1,0:T(4,128)S(1)} %broadcast_select_fusion.10), channel_id=1, source_target_pairs={{0,8},{8,16},{16,24},{24,32},{32,40},{40,48},{48,56},{56,64},{64,7... | collective-permute-start | bytes 98312 | tf_op jit(solution)/shard_map/ppermute | solution.py:15
  94.9 12.9 %collective-permute-start.10 = (f32[4,2048]{1,0:T(4,128)S(1)}, f32[4,2048]{1,0:T(4,128)S(1)}, u32[]{:S(2)}, u32[]{:S(2)}) collective-permute-start(f32[4,2048]{1,0:T(4,128)S(1)} %broadcast_select_fusion.4), channel_id=1, source_target_pairs={{0,1},{1,2},{2,3},{3,4},{4,5},{5,6},{6,7},{8,9},{9,10},{10,11},{11... | collective-permute-start | bytes 98312 | tf_op jit(solution)/shard_map/ppermute | solution.py:15
  99.5 8.3 %collective-permute-start.11 = (f32[4,2048]{1,0:T(4,128)S(1)}, f32[4,2048]{1,0:T(4,128)S(1)}, u32[]{:S(2)}, u32[]{:S(2)}) collective-permute-start(f32[4,2048]{1,0:T(4,128)S(1)} %broadcast_select_fusion.3), channel_id=1, source_target_pairs={{1,0},{2,1},{3,2},{4,3},{5,4},{6,5},{7,6},{9,8},{10,9},{11,10},{12... | collective-permute-start | bytes 98312 | tf_op jit(solution)/shard_map/ppermute | solution.py:15
  101.5 6.3 %collective-permute-start.9 = (f32[4,2048]{1,0:T(4,128)S(1)}, f32[4,2048]{1,0:T(4,128)S(1)}, u32[]{:S(2)}, u32[]{:S(2)}) collective-permute-start(f32[4,2048]{1,0:T(4,128)S(1)} %broadcast_select_fusion.5), channel_id=1, source_target_pairs={{8,0},{16,8},{24,16},{32,24},{40,32},{48,40},{56,48},{64,56},{72,6... | collective-permute-start | bytes 98312 | tf_op jit(solution)/shard_map/ppermute | solution.py:15
  102.9 5.6 %collective-permute-start.8 = (f32[4,2048]{1,0:T(4,128)S(1)}, f32[4,2048]{1,0:T(4,128)S(1)}, u32[]{:S(2)}, u32[]{:S(2)}) collective-permute-start(f32[4,2048]{1,0:T(4,128)S(1)} %broadcast_select_fusion.6), channel_id=1, source_target_pairs={{0,8},{8,16},{16,24},{24,32},{32,40},{40,48},{48,56},{56,64},{64,7... | collective-permute-start | bytes 98312 | tf_op jit(solution)/shard_map/ppermute | solution.py:15
Sparse Core Ops, SparseCore 0:
  134.5 250.0 all-reduce.1
where the time goes:
time: 416 us; the launch traced here: 415 us
  waiting for transfers between devices  252 us (61%)
  matrix products  42.2 us (10%)
  local copies, waits for them, and re-layouts  41.9 us (10%)
  starting transfers between devices  35.5 us (9%)
  other arithmetic  29.4 us (7%)
  between operations  14.5 us (3%)
    psum x1, waiting for transfers between devices, on_device(): gram_total = lax.psum(local_gram, ('fx', 'fy'))  250 us
    dot_general x3, matrix products, contract(): jnp.einsum('fkab,fkbr->far', block_mats, shaped, precision=lax.Precision....  36.3 us
    ppermute x12, starting transfers between devices, from_behind(): return lax.ppermute(block, axis, route)  35.5 us
    reshape x3, local copies, waits for them, and re-layouts, contract(): shaped = picked.reshape(face_count, picked.shape[1], DOF, NRHS)  13.9 us
    another operation x3, other arithmetic, solve_small(): factor = jnp.linalg.cholesky(normal_matrix)  9.45 us
    select_n x4, other arithmetic, on_device(): jnp.take(extended, face_columns, axis=0)  8.94 us
  transfers between devices with their start and end apart: 13, of which 3 were waited for; matrix products, arithmetic and copies ran while one was open for 3% of the time, Pallas kernels for 0%

commit v1 on v0

--- a/solution.py
+++ b/solution.py
@@ -63,7 +63,7 @@
         fields.append(contract(block_mats, jnp.take(extended, face_columns, axis=0)))
     stacked = jnp.concatenate([as_rows(item) for item in fields], axis=1)
     local_gram = jnp.dot(stacked.T, stacked, precision=high, preferred_element_type=jnp.float32)
-    gram_total = lax.psum(local_gram, ("fx", "fy"))
+    gram_total = lax.psum(lax.psum(local_gram, "fx"), "fy")
     coeffs, combo = solve_small(gram_total)
     solution = jnp.dot(stacked[:, : POWERS * NRHS], coeffs, precision=high)
     residual = jnp.dot(stacked, combo, precision=high)

time: 416 us -> 381 us (0.916)
  waiting for transfers between devices: 252 us -> 215 us
    psum x1 -> x2, waiting for transfers between devices: 250 us -> 213 us  [on_device(): gram_total = lax.psum(lax.psum(local_gram, 'fx'), 'fy')]
  transfers between devices with their start and end apart: 13 -> 14, of which waited for: 3 -> 4; matrix products, arithmetic and copies ran while one was open for 3% -> 3% of each run, Pallas kernels for 0% -> 0%
where the time goes in v1:
time: 381 us; the launch traced here: 378 us
  waiting for transfers between devices  215 us (56%)
  matrix products  42 us (11%)
  local copies, waits for them, and re-layouts  41.9 us (11%)
  starting transfers between devices  35.8 us (9%)
  other arithmetic  29.4 us (8%)
  between operations  14.5 us (4%)
    psum x2, waiting for transfers between devices, on_device(): gram_total = lax.psum(lax.psum(local_gram, 'fx'), 'fy')  213 us
    dot_general x3, matrix products, contract(): jnp.einsum('fkab,fkbr->far', block_mats, shaped, precision=lax.Precision....  36 us
    ppermute x12, starting transfers between devices, from_behind(): return lax.ppermute(block, axis, route)  35.5 us
    reshape x3, local copies, waits for them, and re-layouts, contract(): shaped = picked.reshape(face_count, picked.shape[1], DOF, NRHS)  13.9 us
    another operation x3, other arithmetic, solve_small(): factor = jnp.linalg.cholesky(normal_matrix)  9.45 us
    select_n x4, other arithmetic, on_device(): jnp.take(extended, face_columns, axis=0)  8.94 us
    gather x6, local copies, waits for them, and re-layouts, on_device(): jnp.take(extended, face_columns, axis=0)  8.28 us
    another operation x2, other arithmetic, solve_small(): coeffs = jax.scipy.linalg.cho_solve((factor, True), right_terms)  8.01 us
  transfers between devices with their start and end apart: 14, of which 4 were waited for; matrix products, arithmetic and copies ran while one was open for 3% of the time, Pallas kernels for 0%

profile of v1, /device:TPU:1, one launch (start us, length us, event | category | flops | bytes accessed | tf_op | source)
XLA Modules:
  0.0 378.3 jit_solution(7321667405650239549)
XLA Ops:
  7.2 0.8 compare_and_fusion.1
  8.1 1.5 gather_fusion
  9.6 3.9 %collective-permute-start = (f32[4,2048]{1,0:T(4,128)S(1)}, f32[4,2048]{1,0:T(4,128)S(1)}, u32[]{:S(2)}, u32[]{:S(2)}) collective-permute-start(f32[4,2048]{1,0:T(4,128)S(1)} %broadcast_select_fusion.14), channel_id=1, source_target_pairs={{0,8},{8,16},{16,24},{24,32},{32,40},{40,48},{48,56},{56,64},{64,7... | collective-permute-start | bytes 98312 | tf_op jit(solution)/shard_map/ppermute | solution.py:15
  13.6 1.5 gather_fusion.1
  15.2 1.3 collective-permute-start.1
  16.5 1.5 gather_fusion.2
  18.0 4.0 %collective-permute-start.2 = (f32[4,2048]{1,0:T(4,128)S(1)}, f32[4,2048]{1,0:T(4,128)S(1)}, u32[]{:S(2)}, u32[]{:S(2)}) collective-permute-start(f32[4,2048]{1,0:T(4,128)S(1)} %broadcast_select_fusion.12), channel_id=1, source_target_pairs={{0,1},{1,2},{2,3},{3,4},{4,5},{5,6},{6,7},{8,9},{9,10},{10,11},{11... | collective-permute-start | bytes 98312 | tf_op jit(solution)/shard_map/ppermute | solution.py:15
  22.1 1.5 gather_fusion.3
  23.7 1.9 collective-permute-start.3
  25.6 0.7 compare_select_fusion
  26.3 0.7 compare_and_fusion
  27.1 5.7 %reshape.61 = f32[16,11,64,64]{3,2,0,1:T(8,128)} reshape(f32[16,11,4096]{2,0,1:T(8,128)} %param.9) | data formatting | bytes 5767168 | tf_op jit(solution)/shard_map/reshape | solution.py:52
  32.9 1.2 gather_fusion.4
  34.1 1.5 reshape.217
  35.6 1.8 broadcast_select_fusion.2
  37.4 3.6 reshape.245
  41.0 12.0 %fusion.6 = f32[16,64,32]{1,2,0:T(8,128)S(1)} fusion(f32[16,11,64,64]{3,2,0,1:T(8,128)} %reshape.61, f32[16,11,64,32]{3,2,1,0:T(8,128)} %reshape.245), kind=kOutput, calls=%fused_computation.21 | convolution fusion | flops 276824064 | bytes 4456448 | tf_op jit(solution)/shard_map/fkab,fkbr->far/dot_general | solution.py:29
  53.2 0.2 reshape.62
  53.4 0.6 gather_fusion.6
  54.0 0.6 gather_fusion.7
  54.6 0.6 gather_fusion.8
  55.2 0.6 gather_fusion.5
  55.8 1.3 collective-permute-start.5
  57.2 3.6 collective-permute-start.6
  60.9 1.9 collective-permute-start.7
  62.9 5.1 %collective-permute-start.4 = (f32[4,2048]{1,0:T(4,128)S(1)}, f32[4,2048]{1,0:T(4,128)S(1)}, u32[]{:S(2)}, u32[]{:S(2)}) collective-permute-start(f32[4,2048]{1,0:T(4,128)S(1)} %broadcast_select_fusion.10), channel_id=1, source_target_pairs={{0,8},{8,16},{16,24},{24,32},{32,40},{40,48},{48,56},{56,64},{64,7... | collective-permute-start | bytes 98312 | tf_op jit(solution)/shard_map/ppermute | solution.py:15
  68.0 0.8 collective-permute-done.4
  68.9 1.2 gather_fusion.9
  70.0 1.6 reshape.229
  71.7 3.2 broadcast_select_fusion.1
  74.9 5.2 %reshape.246 = f32[16,11,64,32]{3,2,1,0:T(8,128)} reshape(f32[16,11,2048]{2,1,0:T(8,128)} %broadcast_select_fusion.1) | data formatting | bytes 2883584 | tf_op jit(solution)/shard_map/reshape | solution.py:28
  80.1 12.0 %fusion.9 = f32[16,64,32]{1,2,0:T(8,128)S(1)} fusion(f32[16,11,64,64]{3,2,0,1:T(8,128)} %reshape.61, f32[16,11,64,32]{3,2,1,0:T(8,128)} %reshape.246), kind=kOutput, calls=%fused_computation.22 | convolution fusion | flops 276824064 | bytes 4456448 | tf_op jit(solution)/shard_map/fkab,fkbr->far/dot_general | solution.py:29
  92.3 0.2 reshape.64
  92.6 0.6 gather_fusion.12
  93.1 0.6 gather_fusion.13
  93.7 0.6 gather_fusion.11
  94.3 0.6 gather_fusion.10
  94.9 4.5 %collective-permute-start.10 = (f32[4,2048]{1,0:T(4,128)S(1)}, f32[4,2048]{1,0:T(4,128)S(1)}, u32[]{:S(2)}, u32[]{:S(2)}) collective-permute-start(f32[4,2048]{1,0:T(4,128)S(1)} %broadcast_select_fusion.4), channel_id=1, source_target_pairs={{0,1},{1,2},{2,3},{3,4},{4,5},{5,6},{6,7},{8,9},{9,10},{10,11},{11... | collective-permute-start | bytes 98312 | tf_op jit(solution)/shard_map/ppermute | solution.py:15
  99.5 1.9 collective-permute-start.11
  101.5 1.3 collective-permute-start.9
  102.9 4.8 %collective-permute-start.8 = (f32[4,2048]{1,0:T(4,128)S(1)}, f32[4,2048]{1,0:T(4,128)S(1)}, u32[]{:S(2)}, u32[]{:S(2)}) collective-permute-start(f32[4,2048]{1,0:T(4,128)S(1)} %broadcast_select_fusion.6), channel_id=1, source_target_pairs={{0,8},{8,16},{16,24},{24,32},{32,40},{40,48},{48,56},{56,64},{64,7... | collective-permute-start | bytes 98312 | tf_op jit(solution)/shard_map/ppermute | solution.py:15
  107.9 0.6 collective-permute-done.8
  108.5 1.2 gather_fusion.14
  109.7 1.6 reshape.241
  111.3 3.2 broadcast_select_fusion
  114.6 5.2 %reshape.247 = f32[16,11,64,32]{3,2,1,0:T(8,128)} reshape(f32[16,11,2048]{2,1,0:T(8,128)} %broadcast_select_fusion) | data formatting | bytes 2883584 | tf_op jit(solution)/shard_map/reshape | solution.py:28
  119.7 12.0 %fusion.12 = f32[16,64,32]{1,2,0:T(8,128)S(1)} fusion(f32[16,11,64,64]{3,2,0,1:T(8,128)} %reshape.61, f32[16,11,64,32]{3,2,1,0:T(8,128)} %reshape.247), kind=kOutput, calls=%fused_computation.23 | convolution fusion | flops 276824064 | bytes 4456448 | tf_op jit(solution)/shard_map/fkab,fkbr->far/dot_general | solution.py:29
  132.0 0.5 pad_maximum_fusion
  132.4 1.6 fusion.37
  134.1 0.3 all-reduce.5.cloned.1.call-start
  134.4 146.8 %all-reduce.3.cloned.1.call-done = f32[128,128]{1,0:T(8,128)} async-done(((f32[128,128]{1,0:T(8,128)}), f32[128,128]{1,0:T(8,128)}) %all-reduce.3.cloned.1.call-update) | async-done | bytes 65552 | tf_op jit(solution)/shard_map/psum | solution.py:66
  281.3 66.4 %all-reduce.5.cloned.1.call-done = f32[128,128]{1,0:T(8,128)} async-done(((f32[128,128]{1,0:T(8,128)}), f32[128,128]{1,0:T(8,128)}) %all-reduce.5.cloned.1.call-update) | async-done | bytes 65552 | tf_op jit(solution)/shard_map/psum | solution.py:66
  347.7 1.0 fusion.34
  348.7 0.2 fusion.32
  349.1 8.8 %cholesky.16 = f32[96,96]{1,0:T(8,128)S(1)} custom-call(f32[96,96]{1,0:T(8,128)S(1)} %fusion.29), custom_call_target="Cholesky" | custom-call | tf_op jit(solution)/shard_map/jit(cholesky)/cholesky | solution.py:44
  357.9 0.6 compare_reduce_fusion
  358.5 0.7 fusion.24
  359.2 7.4 %custom-call.10 = f32[1,96,96]{1,2,0:T(8,128)S(1)} custom-call(f32[1,96,96]{2,1,0:T(8,128)S(1)} %fusion.24), custom_call_target="InvertDiagBlocksLowerTriangular" | custom-call | tf_op jit(solution)/shard_map/jit(_cho_solve)/triangular_solve | solution.py:45
  366.6 1.1 fusion.21
  367.7 0.3 fusion.27
  368.3 0.7 fusion.15
  369.1 0.6 fusion.38
  369.7 0.9 reshape.67
  370.5 0.9 reshape.66
  (46 shorter events, 2.7 us)
Async XLA Ops:
  7.2 274.1 %all-reduce.3.cloned.1.call-start = ((), (), s32[]{:S(2)}) async-start(), calls=%async_computation | async-start | bytes 131072 | tf_op jit(solution)/shard_map/psum | solution.py:66
  9.6 23.2 %collective-permute-start = (f32[4,2048]{1,0:T(4,128)S(1)}, f32[4,2048]{1,0:T(4,128)S(1)}, u32[]{:S(2)}, u32[]{:S(2)}) collective-permute-start(f32[4,2048]{1,0:T(4,128)S(1)} %broadcast_select_fusion.14), channel_id=1, source_target_pairs={{0,8},{8,16},{16,24},{24,32},{32,40},{40,48},{48,56},{56,64},{64,7... | collective-permute-start | bytes 98312 | tf_op jit(solution)/shard_map/ppermute | solution.py:15
  15.2 17.6 %collective-permute-start.1 = (f32[4,2048]{1,0:T(4,128)S(1)}, f32[4,2048]{1,0:T(4,128)S(1)}, u32[]{:S(2)}, u32[]{:S(2)}) collective-permute-start(f32[4,2048]{1,0:T(4,128)S(1)} %broadcast_select_fusion.13), channel_id=1, source_target_pairs={{8,0},{16,8},{24,16},{32,24},{40,32},{48,40},{56,48},{64,56},{72,6... | collective-permute-start | bytes 98312 | tf_op jit(solution)/shard_map/ppermute | solution.py:15
  18.0 14.8 %collective-permute-start.2 = (f32[4,2048]{1,0:T(4,128)S(1)}, f32[4,2048]{1,0:T(4,128)S(1)}, u32[]{:S(2)}, u32[]{:S(2)}) collective-permute-start(f32[4,2048]{1,0:T(4,128)S(1)} %broadcast_select_fusion.12), channel_id=1, source_target_pairs={{0,1},{1,2},{2,3},{3,4},{4,5},{5,6},{6,7},{8,9},{9,10},{10,11},{11... | collective-permute-start | bytes 98312 | tf_op jit(solution)/shard_map/ppermute | solution.py:15
  23.7 9.2 %collective-permute-start.3 = (f32[4,2048]{1,0:T(4,128)S(1)}, f32[4,2048]{1,0:T(4,128)S(1)}, u32[]{:S(2)}, u32[]{:S(2)}) collective-permute-start(f32[4,2048]{1,0:T(4,128)S(1)} %broadcast_select_fusion.11), channel_id=1, source_target_pairs={{1,0},{2,1},{3,2},{4,3},{5,4},{6,5},{7,6},{9,8},{10,9},{11,10},{12... | collective-permute-start | bytes 98312 | tf_op jit(solution)/shard_map/ppermute | solution.py:15
  27.1 5.7 %copy-start = (f32[16,2048]{1,0:T(8,128)S(1)}, f32[16,2048]{1,0:T(8,128)}, u32[]{:S(2)}) copy-start(f32[16,2048]{1,0:T(8,128)} %param.8) | copy-start | bytes 393220
  55.8 12.2 %collective-permute-start.5 = (f32[4,2048]{1,0:T(4,128)S(1)}, f32[4,2048]{1,0:T(4,128)S(1)}, u32[]{:S(2)}, u32[]{:S(2)}) collective-permute-start(f32[4,2048]{1,0:T(4,128)S(1)} %broadcast_select_fusion.9), channel_id=1, source_target_pairs={{8,0},{16,8},{24,16},{32,24},{40,32},{48,40},{56,48},{64,56},{72,6... | collective-permute-start | bytes 98312 | tf_op jit(solution)/shard_map/ppermute | solution.py:15
  57.2 10.8 %collective-permute-start.6 = (f32[4,2048]{1,0:T(4,128)S(1)}, f32[4,2048]{1,0:T(4,128)S(1)}, u32[]{:S(2)}, u32[]{:S(2)}) collective-permute-start(f32[4,2048]{1,0:T(4,128)S(1)} %broadcast_select_fusion.8), channel_id=1, source_target_pairs={{0,1},{1,2},{2,3},{3,4},{4,5},{5,6},{6,7},{8,9},{9,10},{10,11},{11... | collective-permute-start | bytes 98312 | tf_op jit(solution)/shard_map/ppermute | solution.py:15
  60.9 7.1 %collective-permute-start.7 = (f32[4,2048]{1,0:T(4,128)S(1)}, f32[4,2048]{1,0:T(4,128)S(1)}, u32[]{:S(2)}, u32[]{:S(2)}) collective-permute-start(f32[4,2048]{1,0:T(4,128)S(1)} %broadcast_select_fusion.7), channel_id=1, source_target_pairs={{1,0},{2,1},{3,2},{4,3},{5,4},{6,5},{7,6},{9,8},{10,9},{11,10},{12... | collective-permute-start | bytes 98312 | tf_op jit(solution)/shard_map/ppermute | solution.py:15
  62.9 5.9 %collective-permute-start.4 = (f32[4,2048]{1,0:T(4,128)S(1)}, f32[4,2048]{1,0:T(4,128)S(1)}, u32[]{:S(2)}, u32[]{:S(2)}) collective-permute-start(f32[4,2048]{1,0:T(4,128)S(1)} %broadcast_select_fusion.10), channel_id=1, source_target_pairs={{0,8},{8,16},{16,24},{24,32},{32,40},{40,48},{48,56},{56,64},{64,7... | collective-permute-start | bytes 98312 | tf_op jit(solution)/shard_map/ppermute | solution.py:15
  94.9 12.9 %collective-permute-start.10 = (f32[4,2048]{1,0:T(4,128)S(1)}, f32[4,2048]{1,0:T(4,128)S(1)}, u32[]{:S(2)}, u32[]{:S(2)}) collective-permute-start(f32[4,2048]{1,0:T(4,128)S(1)} %broadcast_select_fusion.4), channel_id=1, source_target_pairs={{0,1},{1,2},{2,3},{3,4},{4,5},{5,6},{6,7},{8,9},{9,10},{10,11},{11... | collective-permute-start | bytes 98312 | tf_op jit(solution)/shard_map/ppermute | solution.py:15
  99.5 8.3 %collective-permute-start.11 = (f32[4,2048]{1,0:T(4,128)S(1)}, f32[4,2048]{1,0:T(4,128)S(1)}, u32[]{:S(2)}, u32[]{:S(2)}) collective-permute-start(f32[4,2048]{1,0:T(4,128)S(1)} %broadcast_select_fusion.3), channel_id=1, source_target_pairs={{1,0},{2,1},{3,2},{4,3},{5,4},{6,5},{7,6},{9,8},{10,9},{11,10},{12... | collective-permute-start | bytes 98312 | tf_op jit(solution)/shard_map/ppermute | solution.py:15
  101.5 6.3 %collective-permute-start.9 = (f32[4,2048]{1,0:T(4,128)S(1)}, f32[4,2048]{1,0:T(4,128)S(1)}, u32[]{:S(2)}, u32[]{:S(2)}) collective-permute-start(f32[4,2048]{1,0:T(4,128)S(1)} %broadcast_select_fusion.5), channel_id=1, source_target_pairs={{8,0},{16,8},{24,16},{32,24},{40,32},{48,40},{56,48},{64,56},{72,6... | collective-permute-start | bytes 98312 | tf_op jit(solution)/shard_map/ppermute | solution.py:15
  102.9 5.6 %collective-permute-start.8 = (f32[4,2048]{1,0:T(4,128)S(1)}, f32[4,2048]{1,0:T(4,128)S(1)}, u32[]{:S(2)}, u32[]{:S(2)}) collective-permute-start(f32[4,2048]{1,0:T(4,128)S(1)} %broadcast_select_fusion.6), channel_id=1, source_target_pairs={{0,8},{8,16},{16,24},{24,32},{32,40},{40,48},{48,56},{56,64},{64,7... | collective-permute-start | bytes 98312 | tf_op jit(solution)/shard_map/ppermute | solution.py:15
  134.1 213.6 %all-reduce.5.cloned.1.call-start = ((), (), s32[]{:S(2)}) async-start(), calls=%async_computation.1 | async-start | bytes 131072 | tf_op jit(solution)/shard_map/psum | solution.py:66
Sparse Core Ops, SparseCore 0:
  134.2 146.9 all-reduce.2
  283.6 64.0 all-reduce.4
